TPU v7x, 256 devices: a whole 4x4x8 slice. The times are simulated.
256 devices in a mesh: member: 8 (over y, x_lo), pix: 32 (over x_hi, z, core).
Axes of the slice: x: 4 (x_hi: 2, x_lo: 2; x = x_hi * 2 + x_lo), y: 4, z: 8, core: 2. Of those that a mesh axis runs over, the one named last changes fastest.
Arguments:
- field: bfloat16 [16, 256, 512, 128], P('member', 'pix'), may hold values from -17 to 17
- dw_kernel: float32 [2, 7, 7, 128], replicated, may hold values from -0.875 to 0.875
- dw_bias: float32 [2, 128], replicated, may hold values from -3 to 3
- ln_gain: float32 [2, 128], replicated, may hold values from 0.25 to 1.75
- w_in: bfloat16 [2, 128, 512], replicated, may hold values from -0.5 to 0.5
- b_in: float32 [2, 512], replicated, may hold values from -3 to 3
- w_out: bfloat16 [2, 512, 128], replicated, may hold values from -0.25 to 0.25
- attn_gain: float32 [128], replicated, may hold values from 0.25 to 1.75
- w_qkv: bfloat16 [128, 384], replicated, may hold values from -11 to 11
- w_proj: bfloat16 [128, 128], replicated, may hold values from -0.5 to 0.5
Outputs:
- refined: bfloat16 [16, 256, 512, 128], P('member', 'pix')
- attended: bfloat16 [16, 32, 64, 128], P('member', 'pix')
All inputs are finite; a program needn't handle non-finite values.
Results may differ from a plain program's by a relative error of at most 0.012.
Values may be sent and summed in bfloat16 or wider, within the bound.
No kernel may reach another device: no remote copies, remote signals or barrier semaphores. Data moves between devices by JAX's collectives and lax.ppermute only.
A program may use at most 64 MiB of HBM per device.

v0:
```python
import jax
import jax.numpy as jnp
from jax import lax
from jax.sharding import PartitionSpec as P

HEADS = 4
POOL = 8


def padded_2(value, sides, width):
    for axis, dim in sides:
        size, length = (lax.axis_size(axis), value.shape[dim])
        up = [(i, (i + 1) % size) for i in range(size - 1)]
        down = [(j, i) for i, j in up]
        last = lax.slice_in_dim(value, length - width, length, axis=dim)
        leading = lax.slice_in_dim(value, 0, width, axis=dim)
        before = lax.ppermute(last, axis, up)
        after = lax.ppermute(leading, axis, down)
        value = jnp.concatenate([before, value, after], axis=dim)
    return value


def in_order(blocks, dim):
    blocks = jnp.moveaxis(blocks, 0, dim)
    shape = blocks.shape
    return blocks.reshape(*shape[:dim], shape[dim] * shape[dim + 1], *shape[dim + 2 :])


def copy_for_each(value, axis):
    copies = jnp.broadcast_to(value, (lax.axis_size(axis), *value.shape))
    return lax.all_to_all(copies, axis, split_axis=0, concat_axis=0, tiled=True)


def collect(value, axis, dim):
    return in_order(copy_for_each(value, axis), dim)


def layer_norm(values, scaling):
    centre = jnp.mean(values, -1, keepdims=True)
    centred = values - centre
    spread = jnp.mean(centred * centred, -1, keepdims=True)
    return centred * lax.rsqrt(spread + 1e-06) * scaling


def depthwise(extended, kernel, offset):
    kernel_side = kernel.shape[0]
    margin = kernel_side // 2
    out_rows = extended.shape[1] - 2 * margin
    columns = extended.shape[2]
    padded = jnp.pad(extended, ((0, 0), (0, 0), (margin, margin), (0, 0)))
    summed = (
        jnp.zeros((extended.shape[0], out_rows, columns, extended.shape[3]), jnp.float32) + offset
    )
    for row_off in range(kernel_side):
        for col_off in range(kernel_side):
            window = padded[:, row_off : row_off + out_rows, col_off : col_off + columns].astype(
                jnp.float32
            )
            summed = summed + window * kernel[row_off, col_off]
    return summed


def convnext(extended, kernel, offset, scaling, w_first, b_first, w_second):
    margin = kernel.shape[0] // 2
    filtered = depthwise(extended, kernel, offset)
    out_shape = filtered.shape
    channels = out_shape[3]
    normed = layer_norm(filtered, scaling).astype(jnp.bfloat16).reshape(-1, channels)
    before = jnp.dot(normed, w_first, preferred_element_type=jnp.float32) + b_first
    hidden = jax.nn.gelu(before, approximate=True).astype(jnp.bfloat16)
    branch = jnp.dot(hidden, w_second, preferred_element_type=jnp.float32).reshape(out_shape)
    centre_rows = extended[:, margin : margin + out_shape[1]].astype(jnp.float32)
    return (centre_rows + branch).astype(jnp.bfloat16)


def on_device(field, dw_kernel, dw_bias, ln_gain, w_in, b_in, w_out, attn_gain, w_qkv, w_proj):
    members, rows, columns, channels = field.shape
    layers = dw_kernel.shape[0]
    margin = dw_kernel.shape[1] // 2
    current = field
    for layer_index in range(layers):
        extended = padded_2(current, (("pix", 1),), margin)
        current = convnext(
            extended,
            dw_kernel[layer_index],
            dw_bias[layer_index],
            ln_gain[layer_index],
            w_in[layer_index],
            b_in[layer_index],
            w_out[layer_index],
        )
    crows = rows // POOL
    ccols = columns // POOL
    cells = crows * ccols
    head_dim = channels // HEADS
    pooled = (
        current.astype(jnp.float32)
        .reshape(members, crows, POOL, ccols, POOL, channels)
        .mean(axis=(2, 4))
    )
    pooled_normed = (
        layer_norm(pooled, attn_gain).astype(jnp.bfloat16).reshape(members * cells, channels)
    )
    all_features = collect(pooled_normed.reshape(members, cells, channels), "member", 0)
    queries = jnp.dot(pooled_normed, w_qkv[:, :channels], preferred_element_type=jnp.float32)
    queries = queries.astype(jnp.bfloat16).reshape(members, cells, channels)
    paired = jnp.dot(
        all_features.reshape(-1, channels), w_qkv[:, channels:], preferred_element_type=jnp.float32
    )
    paired = paired.astype(jnp.bfloat16).reshape(-1, cells, 2 * channels)
    keys_all = paired[:, :, :channels]
    values_all = paired[:, :, channels:]
    queries = queries.reshape(members, cells, HEADS, head_dim)
    keys_all = keys_all.reshape(-1, cells, HEADS, head_dim)
    values_all = values_all.reshape(-1, cells, HEADS, head_dim)
    scores = jnp.einsum("mphd,nphd->mpnh", queries, keys_all, preferred_element_type=jnp.float32)
    scores = scores / jnp.sqrt(jnp.float32(head_dim))
    weights = jax.nn.softmax(scores, axis=2).astype(jnp.bfloat16)
    blended = jnp.einsum("mpnh,nphd->mphd", weights, values_all, preferred_element_type=jnp.float32)
    blended = blended.astype(jnp.bfloat16).reshape(members * cells, channels)
    mixed = jnp.dot(blended, w_proj, preferred_element_type=jnp.float32)
    attended = (pooled.reshape(members * cells, channels) + mixed).astype(jnp.bfloat16)
    return (current, attended.reshape(members, crows, ccols, channels))


def solution(mesh):
    placed = (P("member", "pix", None, None), P(), P(), P(), P(), P(), P(), P(), P(), P())
    return jax.shard_map(
        on_device,
        mesh=mesh,
        in_specs=placed,
        out_specs=(P("member", "pix", None, None), P("member", "pix", None, None)),
        check_vma=False,
    )
```

profile of v0, /device:TPU:4, one launch (start us, length us, event | category | flops | bytes accessed | tf_op | source)
XLA Modules:
  0.0 190.2 jit_solution(14649602924884747839)
XLA Ops:
  0.7 1.6 fusion.100
  2.3 1.9 %collective-permute-start = (bf16[2,3,512,128]{3,2,1,0:T(8,128)(2,1)S(1)}, bf16[2,3,512,128]{3,2,1,0:T(8,128)(2,1)S(1)}, u32[]{:S(2)}, u32[]{:S(2)}) collective-permute-start(bf16[2,3,512,128]{3,2,1,0:T(8,128)(2,1)S(1)} %get-tuple-element.16), channel_id=1, source_target_pairs={{0,1},{1,2},{2,3},{3,4},{4,5},{5,6},{6,7},{7,8},{8,9},{9,10},{10,1... | collective-permute-start | bytes 2359304 | tf_op jit(solution)/shard_map/ppermute | solution.py:17
  4.2 7.3 %collective-permute-start.1 = (bf16[2,3,512,128]{3,2,1,0:T(8,128)(2,1)S(1)}, bf16[2,3,512,128]{3,2,1,0:T(8,128)(2,1)S(1)}, u32[]{:S(2)}, u32[]{:S(2)}) collective-permute-start(bf16[2,3,512,128]{3,2,1,0:T(8,128)(2,1)S(1)} %get-tuple-element.17), channel_id=1, source_target_pairs={{1,0},{2,1},{3,2},{4,3},{5,4},{6,5},{7,6},{8,7},{9,8},{10,9},{11,1... | collective-permute-start | bytes 2359304 | tf_op jit(solution)/shard_map/ppermute | solution.py:18
  14.7 4.5 %collective-permute-done = bf16[2,3,512,128]{3,2,1,0:T(8,128)(2,1)S(1)} collective-permute-done((bf16[2,3,512,128]{3,2,1,0:T(8,128)(2,1)S(1)}, bf16[2,3,512,128]{3,2,1,0:T(8,128)(2,1)S(1)}, u32[]{:S(2)}, u32[]{:S(2)}) %collective-permute-start) | collective-permute-done | bytes 786464 | tf_op jit(solution)/shard_map/ppermute | solution.py:17
  19.3 2.7 %constant_dynamic-update-slice_fusion = (bf16[2,11,512,128]{3,2,1,0:T(8,128)(2,1)S(1)}, bf16[2,11,512,128]{3,2,1,0:T(8,128)(2,1)}) fusion(bf16[2,11,512,128]{3,2,1,0:T(8,128)(2,1)S(1)} %constant_dynamic-update-slice_fusion.1, bf16[2,8,512,128]{3,2,1,0:T(8,128)(2,1)S(1)} %copy-done.1), kind=kLoop, calls=%fused_computation.138 | loop fusion | bytes 6291456 | tf_op jit(solution)/shard_map/concatenate | solution.py:19
  21.9 2.8 %select_maximum_fusion.2 = bf16[2,14,518,128]{3,2,1,0:T(8,128)(2,1)} fusion(bf16[2,3,512,128]{3,2,1,0:T(8,128)(2,1)S(1)} %collective-permute-done.1, bf16[2,8,512,128]{3,2,1,0:T(8,128)(2,1)S(1)} %copy-done.1, bf16[2,3,512,128]{3,2,1,0:T(8,128)(2,1)S(1)} %collective-permute-done), kind=kLoop, calls=%fused_computation.85 | loop fusion | flops 22278144 | bytes 7383040 | tf_op jit(solution)/shard_map/concatenate | solution.py:19
  25.8 60.5 %fusion.97 = (f32[2,8,512]{2,1,0:T(8,128)S(1)}, f32[2,8,512,128]{3,2,1,0:T(8,128)}) fusion(f32[128]{0:T(128)S(1)} %get-tuple-element.74, bf16[2,14,518,128]{3,2,1,0:T(8,128)(2,1)} %select_maximum_fusion.2, f32[128]{0:T(128)S(1)} %get-tuple-element.75, f32[128]{0:T(128)S(1)} %get-tuple-element.76, f32[128]{0:T(128)S(1)} %get-tuple-element.77, ...), kind=kLoop, calls=%fused_computation.248 | loop fusion | flops 155181056 | bytes 107013120 | tf_op jit(solution)/shard_map/reduce_sum | solution.py:39
  86.3 4.1 %multiply_reduce_fusion.1 = f32[2,8,512]{2,1,0:T(8,128)S(1)} fusion(f32[2,8,512,128]{3,2,1,0:T(8,128)} %get-tuple-element.11, f32[2,8,512]{2,1,0:T(8,128)S(1)} %broadcast_multiply_fusion.2), kind=kLoop, calls=%fused_computation.82 | loop fusion | flops 3137536 | bytes 4259840 | tf_op jit(solution)/shard_map/reduce_sum | solution.py:41
  90.5 2.5 %multiply_convert_fusion.1 = bf16[2,8,512,128]{3,2,1,0:T(8,128)(2,1)S(1)} fusion(f32[2,8,512,128]{3,2,1,0:T(8,128)S(1)} %copy-done.2, f32[128]{0:T(128)S(1)} %get-tuple-element.125, f32[2,8,512]{2,1,0:T(8,128)S(1)} %add_rsqrt_fusion.1, f32[2,8,512]{2,1,0:T(8,128)S(1)} %broadcast_multiply_fusion.2), kind=kLoop, calls=%fused_computation.81 | loop fusion | flops 4194304 | bytes 6357504 | tf_op jit(solution)/shard_map/convert_element_type | solution.py:68
  93.0 6.4 %fusion.8 = bf16[8192,512]{1,0:T(8,128)(2,1)S(1)} fusion(bf16[8192,128]{1,0:T(8,128)(2,1)S(1)} %bitcast.277, f32[512]{0:T(512)S(1)} %bitcast.285, bf16[2,128,512]{2,1,0:T(8,128)(2,1)S(1)} %copy-done.7), kind=kOutput, calls=%fused_computation.10 | convolution fusion | flops 1115684864 | bytes 10618880 | tf_op jit(solution)/shard_map/dot_general | solution.py:69
  99.4 2.4 %fusion.43 = bf16[2,8,512,128]{3,2,1,0:T(8,128)(2,1)S(1)} fusion(bf16[2,8,512,128]{3,2,1,0:T(8,128)(2,1)S(1)} %copy-done.1, bf16[2,8,512,512]{3,2,1,0:T(8,128)(2,1)S(1)} %bitcast.274, bf16[2,512,128]{2,1,0:T(8,128)(2,1)S(1)} %copy-done.4), kind=kOutput, calls=%fused_computation.51 | convolution fusion | flops 1076887552 | bytes 12713984 | tf_op jit(solution)/shard_map/dot_general | solution.py:71
  102.0 1.9 %collective-permute-start.2 = (bf16[2,3,512,128]{3,2,1,0:T(8,128)(2,1)S(1)}, bf16[2,3,512,128]{3,2,1,0:T(8,128)(2,1)S(1)}, u32[]{:S(2)}, u32[]{:S(2)}) collective-permute-start(bf16[2,3,512,128]{3,2,1,0:T(8,128)(2,1)S(1)} %get-tuple-element.12), channel_id=1, source_target_pairs={{0,1},{1,2},{2,3},{3,4},{4,5},{5,6},{6,7},{7,8},{8,9},{9,10},{10,1... | collective-permute-start | bytes 2359304 | tf_op jit(solution)/shard_map/ppermute | solution.py:17
  103.9 7.3 %collective-permute-start.3 = (bf16[2,3,512,128]{3,2,1,0:T(8,128)(2,1)S(1)}, bf16[2,3,512,128]{3,2,1,0:T(8,128)(2,1)S(1)}, u32[]{:S(2)}, u32[]{:S(2)}) collective-permute-start(bf16[2,3,512,128]{3,2,1,0:T(8,128)(2,1)S(1)} %get-tuple-element.13), channel_id=1, source_target_pairs={{1,0},{2,1},{3,2},{4,3},{5,4},{6,5},{7,6},{8,7},{9,8},{10,9},{11,1... | collective-permute-start | bytes 2359304 | tf_op jit(solution)/shard_map/ppermute | solution.py:18
  111.2 7.7 %collective-permute-done.2 = bf16[2,3,512,128]{3,2,1,0:T(8,128)(2,1)S(1)} collective-permute-done((bf16[2,3,512,128]{3,2,1,0:T(8,128)(2,1)S(1)}, bf16[2,3,512,128]{3,2,1,0:T(8,128)(2,1)S(1)}, u32[]{:S(2)}, u32[]{:S(2)}) %collective-permute-start.2) | collective-permute-done | bytes 786464 | tf_op jit(solution)/shard_map/ppermute | solution.py:17
  118.9 1.8 collective-permute-done.3
  121.9 32.1 %fusion.95 = (f32[2,8,512]{2,1,0:T(8,128)S(1)}, f32[2,8,512,128]{3,2,1,0:T(8,128)S(1)}) fusion(f32[128]{0:T(128)S(1)} %get-tuple-element.25, bf16[2,14,518,128]{3,2,1,0:T(8,128)(2,1)S(1)} %select_maximum_fusion, f32[128]{0:T(128)S(1)} %get-tuple-element.26, f32[128]{0:T(128)S(1)} %get-tuple-element.27, f32[128]{0:T(128)S(1)} %get-tuple-element.28, ...), kind=kLoop, calls=%fused_computation.247 | loop fusion | flops 161472512 | bytes 96003072 | tf_op jit(solution)/shard_map/reduce_sum | solution.py:39
  154.0 2.4 %multiply_reduce_fusion = f32[2,8,512]{2,1,0:T(8,128)S(1)} fusion(f32[2,8,512,128]{3,2,1,0:T(8,128)S(1)} %get-tuple-element.9, f32[2,8,512]{2,1,0:T(8,128)S(1)} %broadcast_multiply_fusion.1), kind=kLoop, calls=%fused_computation.80 | loop fusion | flops 3137536 | bytes 4259840 | tf_op jit(solution)/shard_map/reduce_sum | solution.py:41
  156.4 2.5 %multiply_convert_fusion = bf16[2,8,512,128]{3,2,1,0:T(8,128)(2,1)S(1)} fusion(f32[2,8,512,128]{3,2,1,0:T(8,128)S(1)} %get-tuple-element.9, f32[128]{0:T(128)S(1)} %get-tuple-element.124, f32[2,8,512]{2,1,0:T(8,128)S(1)} %add_rsqrt_fusion, f32[2,8,512]{2,1,0:T(8,128)S(1)} %broadcast_multiply_fusion.1), kind=kLoop, calls=%fused_computation.79 | loop fusion | flops 4194304 | bytes 6357504 | tf_op jit(solution)/shard_map/convert_element_type | solution.py:68
  158.9 6.2 %fusion.16 = bf16[8192,512]{1,0:T(8,128)(2,1)S(1)} fusion(bf16[8192,128]{1,0:T(8,128)(2,1)S(1)} %bitcast.276, f32[512]{0:T(512)S(1)} %bitcast.284, bf16[2,128,512]{2,1,0:T(8,128)(2,1)S(1)} %copy-done.7), kind=kOutput, calls=%fused_computation.18 | convolution fusion | flops 1115684864 | bytes 10618880 | tf_op jit(solution)/shard_map/dot_general | solution.py:69
  165.2 3.7 %convert_reduce_fusion = (f32[2,512,128]{2,1,0:T(8,128)S(1)}, bf16[2,8,512,128]{3,2,1,0:T(8,128)(2,1)}) fusion(bf16[2,8,512,512]{3,2,1,0:T(8,128)(2,1)S(1)} %bitcast.275, bf16[2,512,128]{2,1,0:T(8,128)(2,1)S(1)} %copy-done.4, bf16[2,8,512,128]{3,2,1,0:T(8,128)(2,1)S(1)} %fusion.43), kind=kOutput, calls=%fused_computation.78 | convolution fusion | flops 1078853632 | bytes 13238272 | tf_op jit(solution)/shard_map/dot_general | solution.py:71
  170.3 5.9 %all-to-all-start = ((bf16[8,2,64,128]{3,2,1,0:T(8,128)(2,1)}), bf16[8,2,64,128]{3,2,1,0:T(8,128)(2,1)S(1)}, u32[]{:S(2)}, u32[]{:S(2)}) async-start(bf16[8,2,64,128]{3,2,1,0:T(8,128)(2,1)} %broadcast_in_dim.2), calls=%async_computation | async-start | bytes 524288 | tf_op jit(solution)/shard_map/all_to_all | solution.py:31
  176.9 6.7 %all-to-all-done = bf16[8,2,64,128]{3,2,1,0:T(8,128)(2,1)S(1)} async-done(((bf16[8,2,64,128]{3,2,1,0:T(8,128)(2,1)}), bf16[8,2,64,128]{3,2,1,0:T(8,128)(2,1)S(1)}, u32[]{:S(2)}, u32[]{:S(2)}) %all-to-all-start) | async-done | bytes 262176 | tf_op jit(solution)/shard_map/all_to_all | solution.py:31
  184.2 1.6 copy.29
  186.1 1.6 copy.31
  (59 shorter events, 11.3 us)
Async XLA Ops:
  0.6 188.8 %copy-start = (bf16[128,128]{1,0:T(8,128)(2,1)S(1)}, bf16[128,128]{1,0:T(8,128)(2,1)}, u32[]{:S(2)}) copy-start(bf16[128,128]{1,0:T(8,128)(2,1)} %param.19) | copy-start | bytes 98308
  0.6 18.6 %copy-start.1 = (bf16[2,8,512,128]{3,2,1,0:T(8,128)(2,1)S(1)}, bf16[2,8,512,128]{3,2,1,0:T(8,128)(2,1)}, u32[]{:S(2)}) copy-start(bf16[2,8,512,128]{3,2,1,0:T(8,128)(2,1)} %param.10) | copy-start | bytes 6291460
  2.3 16.9 %collective-permute-start = (bf16[2,3,512,128]{3,2,1,0:T(8,128)(2,1)S(1)}, bf16[2,3,512,128]{3,2,1,0:T(8,128)(2,1)S(1)}, u32[]{:S(2)}, u32[]{:S(2)}) collective-permute-start(bf16[2,3,512,128]{3,2,1,0:T(8,128)(2,1)S(1)} %get-tuple-element.16), channel_id=1, source_target_pairs={{0,1},{1,2},{2,3},{3,4},{4,5},{5,6},{6,7},{7,8},{8,9},{9,10},{10,1... | collective-permute-start | bytes 2359304 | tf_op jit(solution)/shard_map/ppermute | solution.py:17
  4.2 17.7 %collective-permute-start.1 = (bf16[2,3,512,128]{3,2,1,0:T(8,128)(2,1)S(1)}, bf16[2,3,512,128]{3,2,1,0:T(8,128)(2,1)S(1)}, u32[]{:S(2)}, u32[]{:S(2)}) collective-permute-start(bf16[2,3,512,128]{3,2,1,0:T(8,128)(2,1)S(1)} %get-tuple-element.17), channel_id=1, source_target_pairs={{1,0},{2,1},{3,2},{4,3},{5,4},{6,5},{7,6},{8,7},{9,8},{10,9},{11,1... | collective-permute-start | bytes 2359304 | tf_op jit(solution)/shard_map/ppermute | solution.py:18
  21.9 3.8 %copy-start.3 = (bf16[2,11,512,128]{3,2,1,0:T(8,128)(2,1)}, bf16[2,11,512,128]{3,2,1,0:T(8,128)(2,1)S(1)}, u32[]{:S(2)}) copy-start(bf16[2,11,512,128]{3,2,1,0:T(8,128)(2,1)S(1)} %get-tuple-element.14) | copy-start | bytes 8650756
  86.3 4.2 %copy-start.2 = (f32[2,8,512,128]{3,2,1,0:T(8,128)S(1)}, f32[2,8,512,128]{3,2,1,0:T(8,128)}, u32[]{:S(2)}) copy-start(f32[2,8,512,128]{3,2,1,0:T(8,128)} %get-tuple-element.11) | copy-start | bytes 12582916
  90.4 2.5 %copy-start.7 = (bf16[2,128,512]{2,1,0:T(8,128)(2,1)S(1)}, bf16[2,128,512]{2,1,0:T(8,128)(2,1)}, u32[]{:S(2)}) copy-start(bf16[2,128,512]{2,1,0:T(8,128)(2,1)} %param.14) | copy-start | bytes 786436
  93.0 6.4 %copy-start.4 = (bf16[2,512,128]{2,1,0:T(8,128)(2,1)S(1)}, bf16[2,512,128]{2,1,0:T(8,128)(2,1)}, u32[]{:S(2)}) copy-start(bf16[2,512,128]{2,1,0:T(8,128)(2,1)} %param.16) | copy-start | bytes 786436
  102.0 16.9 %collective-permute-start.2 = (bf16[2,3,512,128]{3,2,1,0:T(8,128)(2,1)S(1)}, bf16[2,3,512,128]{3,2,1,0:T(8,128)(2,1)S(1)}, u32[]{:S(2)}, u32[]{:S(2)}) collective-permute-start(bf16[2,3,512,128]{3,2,1,0:T(8,128)(2,1)S(1)} %get-tuple-element.12), channel_id=1, source_target_pairs={{0,1},{1,2},{2,3},{3,4},{4,5},{5,6},{6,7},{7,8},{8,9},{9,10},{10,1... | collective-permute-start | bytes 2359304 | tf_op jit(solution)/shard_map/ppermute | solution.py:17
  103.9 16.8 %collective-permute-start.3 = (bf16[2,3,512,128]{3,2,1,0:T(8,128)(2,1)S(1)}, bf16[2,3,512,128]{3,2,1,0:T(8,128)(2,1)S(1)}, u32[]{:S(2)}, u32[]{:S(2)}) collective-permute-start(bf16[2,3,512,128]{3,2,1,0:T(8,128)(2,1)S(1)} %get-tuple-element.13), channel_id=1, source_target_pairs={{1,0},{2,1},{3,2},{4,3},{5,4},{6,5},{7,6},{8,7},{9,8},{10,9},{11,1... | collective-permute-start | bytes 2359304 | tf_op jit(solution)/shard_map/ppermute | solution.py:18
  165.1 4.4 %copy-start.6 = (f32[128]{0:T(128)S(1)}, f32[128]{0:T(128)}, u32[]{:S(2)}) copy-start(f32[128]{0:T(128)} %param.17) | copy-start | bytes 1540
  165.1 11.2 %copy-start.5 = (bf16[128,384]{1,0:T(8,128)(2,1)S(1)}, bf16[128,384]{1,0:T(8,128)(2,1)}, u32[]{:S(2)}) copy-start(bf16[128,384]{1,0:T(8,128)(2,1)} %param.18) | copy-start | bytes 294916
  170.3 13.2 %all-to-all-start = ((bf16[8,2,64,128]{3,2,1,0:T(8,128)(2,1)}), bf16[8,2,64,128]{3,2,1,0:T(8,128)(2,1)S(1)}, u32[]{:S(2)}, u32[]{:S(2)}) async-start(bf16[8,2,64,128]{3,2,1,0:T(8,128)(2,1)} %broadcast_in_dim.2), calls=%async_computation | async-start | bytes 524288 | tf_op jit(solution)/shard_map/all_to_all | solution.py:31
where the time goes:
time: 191 us; the launch traced here: 190 us
  other arithmetic  109 us (57%)
  starting transfers between devices  24.2 us (13%)
  matrix products  21.5 us (11%)
  waiting for transfers between devices  20.6 us (11%)
  local copies, waits for them, and re-layouts  14.2 us (7%)
    reduce_sum x3, other arithmetic, layer_norm(): centre = jnp.mean(values, -1, keepdims=True)  92.7 us
    ppermute x2, starting transfers between devices, padded_2(): after = lax.ppermute(leading, axis, down)  14.5 us
    dot_general x2, matrix products, convnext(): jnp.dot(normed, w_first, preferred_element_type=jnp.float32) + b_first  12.6 us
    ppermute x2, waiting for transfers between devices, padded_2(): before = lax.ppermute(last, axis, up)  12.1 us
    reduce_sum x3, other arithmetic, layer_norm(): spread = jnp.mean(centred * centred, -1, keepdims=True)  6.68 us
    all_to_all x1, waiting for transfers between devices, copy_for_each(): return lax.all_to_all(copies, axis, split_axis=0, concat_axis=0, tiled=True)  6.67 us
    dot_general x2, matrix products, convnext(): jnp.dot(hidden, w_second, preferred_element_type=jnp.float32)  6.18 us
    all_to_all x1, starting transfers between devices, copy_for_each(): return lax.all_to_all(copies, axis, split_axis=0, concat_axis=0, tiled=True)  5.9 us
  transfers between devices with their start and end apart: 5, of which 4 were waited for; matrix products, arithmetic and copies ran while one was open for 3% of the time, Pallas kernels for 0%

commit v1 on v0

v1 whole, which is shorter than its diff:
```python
import functools

import jax
import jax.numpy as jnp
from jax import lax
from jax.experimental import pallas as pl
from jax.experimental.pallas import tpu as pltpu
from jax.sharding import PartitionSpec as P

bf16, f32 = jnp.bfloat16, jnp.float32
HEADS = 4
POOL = 8
KS = 7
PAD = KS // 2
C = 128
JB = 8


def fill_edges(xs, row, run):
    sub = lax.broadcasted_iota(jnp.int32, (8, C), 0)
    for q in range(PAD):
        v = xs[row, run + q].astype(f32)
        a, b = pltpu.roll(v[:, :C], 1, 0), pltpu.roll(v[:, C:], 1, 0)
        v = jnp.concatenate([jnp.where(sub == 0, 0.0, a), jnp.where(sub == 0, a, b)], 1)
        xs[row, q] = v.astype(bf16)
        v = xs[row, PAD + q].astype(f32)
        a, b = pltpu.roll(v[:, :C], 7, 0), pltpu.roll(v[:, C:], 7, 0)
        v = jnp.concatenate([jnp.where(sub == 7, b, a), jnp.where(sub == 7, 0.0, b)], 1)
        xs[row, PAD + run + q] = v.astype(bf16)


def block_kernel(first, layer, rows, run, n_in, *refs):
    x_ref, top_ref, bot_ref, dwk_ref, dwb_ref, gain_ref, w1_ref, b1_ref, w2_ref = refs[:9]
    if first:
        y_ref, ytop_ref, ybot_ref, xs, kb, w2s, xf = refs[n_in:]
    else:
        attn_ref = refs[9]
        y_ref, pool_ref, normed_ref, xs, kb, w2s, xf, acc = refs[n_in:]
    r = pl.program_id(1)

    @pl.when(r == 0)
    def _():
        for t in range(KS * KS):
            k = jnp.broadcast_to(dwk_ref[0, t // KS, pl.ds(t % KS, 1), :], (8, C))
            kb[t] = jnp.concatenate([k, k], 1).astype(bf16)
        w2s[...] = w2_ref[0] * bf16(0.5)

        def put(src, i, row):
            if first:
                xf[...] = src[0, i].astype(f32)
                for j in range(run):
                    a = xf[pl.ds(j, 8, stride=run), :]
                    b = xf[pl.ds(8 * run + j, 8, stride=run), :]
                    xs[row, PAD + j] = jnp.concatenate([a, b], 1).astype(bf16)
            else:
                xs[row, PAD:PAD + run] = src[0, i]
            fill_edges(xs, row, run)

        def edge(i, _):
            put(top_ref, i, i)
            put(bot_ref, i, i + PAD + rows)
            return 0

        def own(i, _):
            put(x_ref, i, i + PAD)
            return 0

        lax.fori_loop(0, PAD, edge, 0)
        lax.fori_loop(0, rows, own, 0)
        if not first:
            acc[...] = jnp.zeros_like(acc)

    bias = dwb_ref[layer:layer + 1, :]
    gain = gain_ref[layer:layer + 1, :]
    b1 = b1_ref[layer:layer + 1, :]
    for jb in range(run // JB):
        tot = [None] * JB
        for dr in range(KS):
            ks = [kb[dr * KS + dw] for dw in range(KS)]
            xv = [xs[r + dr, jb * JB + q] for q in range(JB + KS - 1)]
            for o in range(JB):
                p = [xv[o + dw] * ks[dw] for dw in range(KS)]
                part = ((p[0] + p[1]) + (p[2] + p[3])) + ((p[4] + p[5]) + p[6])
                tot[o] = part if tot[o] is None else tot[o] + part
        tf = [t.astype(f32) for t in tot]
        f = jnp.concatenate([t[:, :C] for t in tf] + [t[:, C:] for t in tf], 0) + bias
        cen = f - jnp.mean(f, -1, keepdims=True)
        var = jnp.mean(cen * cen, -1, keepdims=True)
        normed = (cen * lax.rsqrt(var + 1e-6) * gain).astype(bf16)
        u = (jnp.dot(normed, w1_ref[0], preferred_element_type=f32) + b1).astype(bf16)
        t = u * (u * u * bf16(0.7978845608 * 0.044715) + bf16(0.7978845608))
        br = jnp.dot(u * jnp.tanh(t) + u, w2s[...], preferred_element_type=f32)
        p = None
        for j in range(JB):
            xc = xs[r + PAD, PAD + jb * JB + j].astype(f32)
            y = xc + jnp.concatenate([br[j * 8:j * 8 + 8], br[(JB + j) * 8:(JB + j) * 8 + 8]], 1)
            y = y.astype(bf16)
            if first:
                y_ref[0, 0, jb * JB + j] = y
            else:
                v = y.astype(f32)
                p = v if p is None else p + v
                xf[pl.ds(jb * JB + j, 8, stride=run), :] = v[:, :C]
                xf[pl.ds(8 * run + jb * JB + j, 8, stride=run), :] = v[:, C:]
        if not first:
            acc[jb] += p
    if first:
        @pl.when(r < PAD)
        def _():
            ytop_ref[0, r] = y_ref[0, 0]

        @pl.when(r >= rows - PAD)
        def _():
            ybot_ref[0, r - (rows - PAD)] = y_ref[0, 0]
    else:
        y_ref[0, 0] = xf[...].astype(bf16)

        @pl.when(r == rows - 1)
        def _():
            v = acc[...].reshape(run // JB * 8, 2 * C) * (1.0 / (POOL * POOL))
            v = jnp.concatenate([v[:, :C], v[:, C:]], 0)
            pool_ref[0] = v
            cen = v - jnp.mean(v, -1, keepdims=True)
            var = jnp.mean(cen * cen, -1, keepdims=True)
            normed_ref[0] = (cen * lax.rsqrt(var + 1e-6) * attn_ref[...]).astype(bf16)


def convnext(first, layer, member, members, x, top, bot, weights, out=None):
    rows = x.shape[1]
    columns = x.shape[2] if first else x.shape[2] * 16
    run = columns // 16
    cells = columns // POOL
    side = (run, 8, 2 * C)
    dwk, dwb, gain, w1, b1, w2, attn_gain = weights

    def part(a, at=0):
        return pl.BlockSpec((1,) + a.shape[1:], lambda m, r: (at,) + (0,) * (a.ndim - 1))

    def whole(a):
        return pl.BlockSpec(a.shape, lambda m, r: (0,) * a.ndim)

    args = [x, top, bot, dwk, dwb, gain, w1, b1, w2]
    specs = [part(x, member if first else 0), part(top), part(bot), part(dwk, layer), whole(dwb), whole(gain),
             part(w1, layer), whole(b1), part(w2, layer)]
    scratch = [
        pltpu.VMEM((rows + 2 * PAD, run + 2 * PAD, 8, 2 * C), bf16),
        pltpu.VMEM((KS * KS, 8, 2 * C), bf16),
        pltpu.VMEM(w2.shape[1:], bf16),
        pltpu.VMEM((columns, C), f32),
    ]
    alias = {}
    if first:
        shapes = [jax.ShapeDtypeStruct((1, rows) + side, bf16)] + [jax.ShapeDtypeStruct((1, PAD) + side, bf16)] * 2
        outs = [pl.BlockSpec((1, 1) + side, lambda m, r: (0, r, 0, 0, 0))]
        outs += [pl.BlockSpec((1, PAD) + side, lambda m, r: (0, 0, 0, 0, 0))] * 2
    else:
        args.append(attn_gain)
        specs.append(whole(attn_gain))
        if out is not None:
            alias = {len(args): 0}
            args.append(out)
            specs.append(pl.BlockSpec(memory_space=pl.ANY))
        shapes = [
            jax.ShapeDtypeStruct((members, rows, columns, C), bf16),
            jax.ShapeDtypeStruct((1, cells, C), f32),
            jax.ShapeDtypeStruct((1, cells, C), bf16),
        ]
        outs = [pl.BlockSpec((1, 1, columns, C), lambda m, r: (member, r, 0, 0))]
        outs += [pl.BlockSpec((1, cells, C), lambda m, r: (0, 0, 0))] * 2
        scratch.append(pltpu.VMEM((run // JB, 8, 2 * C), f32))
    positions = rows * columns
    return pl.pallas_call(
        functools.partial(block_kernel, first, layer, rows, run, len(args)),
        out_shape=shapes,
        grid=(1, rows),
        in_specs=specs,
        out_specs=outs,
        scratch_shapes=scratch,
        input_output_aliases=alias,
        name="convnext_first" if first else "convnext_last",
        compiler_params=pltpu.CompilerParams(vmem_limit_bytes=40 << 20),
        cost_estimate=pl.CostEstimate(
            flops=positions * C * (4 * 512 + 98), bytes_accessed=4 * positions * C, transcendentals=positions * 512
        ),
    )(*args)


def attention_kernel(members, total, cells, feats_ref, own_ref, pool_ref, wqkv_ref, wproj_ref, out_ref, order):
    wqkv = wqkv_ref[...]
    own = jnp.concatenate([own_ref[m] for m in range(members)], 0)
    q = jnp.dot(own, wqkv[:, :C], preferred_element_type=f32).astype(bf16).astype(f32)
    feats = feats_ref[...].reshape(total * cells, C)
    kv = jnp.dot(feats, wqkv[:, C:], preferred_element_type=f32).astype(bf16).astype(f32)
    head = C // HEADS
    row_head = lax.broadcasted_iota(jnp.int32, (2 * C, C), 0) % C // head
    col_head = lax.broadcasted_iota(jnp.int32, (2 * C, C), 1) // head
    ones = jnp.where(row_head == col_head, 1.0, 0.0).astype(bf16)
    blended = []
    for m in range(members):
        qm = q[m * cells:(m + 1) * cells]
        scores = []
        for n in range(total):
            prod = qm * kv[n * cells:(n + 1) * cells, :C]
            high = prod.astype(bf16)
            low = (prod - high.astype(f32)).astype(bf16)
            both = jnp.concatenate([high, low], 1)
            scores.append(jnp.dot(both, ones, preferred_element_type=f32) * (1.0 / head ** 0.5))
        most = functools.reduce(jnp.maximum, scores)
        exps = [jnp.exp(s - most) for s in scores]
        inverse = 1.0 / functools.reduce(jnp.add, exps)
        mix = None
        for n in range(total):
            w = (exps[n] * inverse).astype(bf16).astype(f32)
            term = w * kv[n * cells:(n + 1) * cells, C:]
            mix = term if mix is None else mix + term
        blended.append(mix.astype(bf16))
    mixed = jnp.dot(jnp.concatenate(blended, 0), wproj_ref[...], preferred_element_type=f32)
    across = cells // 16
    for m in range(members):
        v = pool_ref[m] + mixed[m * cells:(m + 1) * cells]
        for i in range(2 * across):
            half, jj = i // across, i % across
            order[pl.ds(half * 8 * across + jj, 8, stride=across), :] = v[i * 8:(i + 1) * 8]
        out_ref[m, 0] = order[...].astype(bf16)


def attend(feats, own, pooled, wqkv, wproj):
    members, cells, _ = own.shape
    vmem = pl.BlockSpec(memory_space=pltpu.VMEM)
    return pl.pallas_call(
        functools.partial(attention_kernel, members, feats.shape[0], cells),
        out_shape=jax.ShapeDtypeStruct((members, 1, cells, C), bf16),
        in_specs=[vmem] * 5,
        out_specs=vmem,
        scratch_shapes=[pltpu.VMEM((cells, C), f32)],
        name="member_attention",
    )(feats, own, pooled, wqkv, wproj)


def gather_members(value):
    copies = jnp.broadcast_to(value, (lax.axis_size("member"), *value.shape))
    return lax.all_to_all(copies, "member", split_axis=0, concat_axis=0, tiled=True)


def on_device(field, dw_kernel, dw_bias, ln_gain, w_in, b_in, w_out, attn_gain, w_qkv, w_proj):
    members, rows, columns, channels = field.shape
    size = lax.axis_size("pix")
    up = [(i, i + 1) for i in range(size - 1)]
    down = [(j, i) for i, j in up]
    weights = (dw_kernel, dw_bias, ln_gain, w_in, b_in, w_out, attn_gain.reshape(1, channels))
    halos = []
    for m in range(members):
        halos.append((
            lax.ppermute(field[m:m + 1, rows - PAD:], "pix", up),
            lax.ppermute(field[m:m + 1, :PAD], "pix", down),
        ))
    middle = []
    for m in range(members):
        y, ytop, ybot = convnext(True, 0, m, members, field, *halos[m], weights)
        middle.append((y, lax.ppermute(ybot, "pix", up), lax.ppermute(ytop, "pix", down)))
    refined, pooled, normed = None, [], []
    for m in range(members):
        refined, p, z = convnext(False, 1, m, members, *middle[m], weights, out=refined)
        pooled.append(p)
        normed.append(z)
    pooled = jnp.concatenate(pooled, 0)
    normed = jnp.concatenate(normed, 0)
    cells = normed.shape[1]
    feats = gather_members(normed).reshape(-1, cells, channels)
    attended = attend(feats, normed, pooled, w_qkv, w_proj)
    return refined, attended


def solution(mesh):
    placed = (P("member", "pix", None, None), P(), P(), P(), P(), P(), P(), P(), P(), P())
    return jax.shard_map(
        on_device,
        mesh=mesh,
        in_specs=placed,
        out_specs=(P("member", "pix", None, None), P("member", "pix", None, None)),
        check_vma=False,
    )
```

time: 191 us -> 108 us (0.57)
  other arithmetic: 109 us -> 0.62 us
  Pallas kernels: 0 us -> 52.2 us
  matrix products: 21.5 us -> 0 us
  starting transfers between devices: 24.2 us -> 42.6 us
  waiting for transfers between devices: 20.6 us -> 8.23 us
  local copies, waits for them, and re-layouts: 14.2 us -> 3.14 us
    reduce_sum x7 -> x0, other arithmetic: 99.5 us -> none  [the longest x3 92.7 us: layer_norm(): centre = jnp.mean(values, -1, keepdims=True)]
    pallas_call x0 -> x5, Pallas kernels: none -> 52.2 us  [the longest x4 49.6 us: convnext(): pl.pallas_call(functools.partial(block_kernel, first, layer, rows, run, l...]
    dot_general x8 -> x0, matrix products: 20.5 us -> none  [the longest x2 12.6 us: convnext(): jnp.dot(normed, w_first, preferred_element_type=jnp.float32) + b_first]
    ppermute x4 -> x8, starting transfers between devices: 18.4 us -> 36.6 us  [the longest x2 14.5 us: on_device(): lax.ppermute(ytop, 'pix', down)]
    ppermute x4 -> x8, waiting for transfers between devices: 13.9 us -> 1.57 us  [the longest x2 1.55 us: on_device(): lax.ppermute(field[m:m + 1, rows - PAD:], 'pix', up)]
    convert_element_type x4 -> x0, other arithmetic: 5.18 us -> none  [the longest x2 4.97 us: convnext(): layer_norm(filtered, scaling).astype(jnp.bfloat16).reshape(-1, channels)]
    concatenate x2 -> x1, local copies, waits for them, and re-layouts: 3.7 us -> 0.01 us  [on_device(): normed = jnp.concatenate(normed, 0)]
    concatenate x2 -> x1, other arithmetic: 4.04 us -> 0.62 us  [on_device(): pooled = jnp.concatenate(pooled, 0)]
  transfers between devices with their start and end apart: 5 -> 9, of which waited for: 4 -> 2; matrix products, arithmetic and copies ran while one was open for 3% -> 1% of each run, Pallas kernels for 0% -> 35%
where the time goes in v1:
time: 108 us
  Pallas kernels  52.2 us (48%)
  starting transfers between devices  42.6 us (39%)
  waiting for transfers between devices  8.23 us (8%)
  local copies, waits for them, and re-layouts  3.14 us (3%)
    pallas_call x4, Pallas kernels, convnext(): pl.pallas_call(functools.partial(block_kernel, first, layer, rows, run, l...  49.6 us
    ppermute x2, starting transfers between devices, on_device(): lax.ppermute(ytop, 'pix', down)  14.5 us
    ppermute x2, starting transfers between devices, on_device(): lax.ppermute(field[m:m + 1, :PAD], 'pix', down)  14.4 us
    all_to_all x1, waiting for transfers between devices, gather_members(): lax.all_to_all(copies, 'member', split_axis=0, concat_axis=0, tiled=True)  6.66 us
    all_to_all x1, starting transfers between devices, gather_members(): lax.all_to_all(copies, 'member', split_axis=0, concat_axis=0, tiled=True)  6 us
    ppermute x2, starting transfers between devices, on_device(): lax.ppermute(ybot, 'pix', up)  3.84 us
    ppermute x2, starting transfers between devices, on_device(): lax.ppermute(field[m:m + 1, rows - PAD:], 'pix', up)  3.84 us
    pallas_call x1, Pallas kernels, attend(): pl.pallas_call(functools.partial(attention_kernel, members, feats.shape[0...  2.58 us
  transfers between devices with their start and end apart: 9, of which 2 were waited for; matrix products, arithmetic and copies ran while one was open for 1% of the time, Pallas kernels for 35%

profile of v1, /device:TPU:4, one launch (start us, length us, event | category | flops | bytes accessed | tf_op | source)
XLA Modules:
  0.0 107.7 jit_solution(2160312679314480293)
XLA Ops:
  0.7 1.6 %fusion = (bf16[1,3,512,128]{3,2,1,0:T(8,128)(2,1)S(1)}, bf16[1,3,512,128]{3,2,1,0:T(8,128)(2,1)S(1)}, bf16[1,3,512,128]{3,2,1,0:T(8,128)(2,1)S(1)}, bf16[1,3,512,128]{3,2,1,0:T(8,128)(2,1)S(1)}) fusion(bf16[2,8,512,128]{3,2,1,0:T(8,128)(2,1)} %refs_0_.3), kind=kLoop, calls=%fused_computation.3 | loop fusion | bytes 3145728 | tf_op jit(solution)/shard_map/slice | solution.py:255
  2.3 7.1 %collective-permute-start.5 = (bf16[1,3,512,128]{3,2,1,0:T(8,128)(2,1)S(1)}, bf16[1,3,512,128]{3,2,1,0:T(8,128)(2,1)S(1)}, u32[]{:S(2)}, u32[]{:S(2)}) collective-permute-start(bf16[1,3,512,128]{3,2,1,0:T(8,128)(2,1)S(1)} %get-tuple-element.26), channel_id=1, source_target_pairs={{1,0},{2,1},{3,2},{4,3},{5,4},{6,5},{7,6},{8,7},{9,8},{10,9},{11,1... | collective-permute-start | bytes 1179656 | tf_op jit(solution)/shard_map/ppermute | solution.py:255
  9.5 1.9 %collective-permute-start.4 = (bf16[1,3,512,128]{3,2,1,0:T(8,128)(2,1)S(1)}, bf16[1,3,512,128]{3,2,1,0:T(8,128)(2,1)S(1)}, u32[]{:S(2)}, u32[]{:S(2)}) collective-permute-start(bf16[1,3,512,128]{3,2,1,0:T(8,128)(2,1)S(1)} %get-tuple-element.27), channel_id=1, source_target_pairs={{0,1},{1,2},{2,3},{3,4},{4,5},{5,6},{6,7},{7,8},{8,9},{9,10},{10,1... | collective-permute-start | bytes 1179656 | tf_op jit(solution)/shard_map/ppermute | solution.py:254
  11.4 7.3 %collective-permute-start.1 = (bf16[1,3,512,128]{3,2,1,0:T(8,128)(2,1)S(1)}, bf16[1,3,512,128]{3,2,1,0:T(8,128)(2,1)S(1)}, u32[]{:S(2)}, u32[]{:S(2)}) collective-permute-start(bf16[1,3,512,128]{3,2,1,0:T(8,128)(2,1)S(1)} %get-tuple-element.28), channel_id=1, source_target_pairs={{1,0},{2,1},{3,2},{4,3},{5,4},{6,5},{7,6},{8,7},{9,8},{10,9},{11,1... | collective-permute-start | bytes 1179656 | tf_op jit(solution)/shard_map/ppermute | solution.py:255
  18.7 1.9 %collective-permute-start = (bf16[1,3,512,128]{3,2,1,0:T(8,128)(2,1)S(1)}, bf16[1,3,512,128]{3,2,1,0:T(8,128)(2,1)S(1)}, u32[]{:S(2)}, u32[]{:S(2)}) collective-permute-start(bf16[1,3,512,128]{3,2,1,0:T(8,128)(2,1)S(1)} %get-tuple-element.29), channel_id=1, source_target_pairs={{0,1},{1,2},{2,3},{3,4},{4,5},{5,6},{6,7},{7,8},{8,9},{9,10},{10,1... | collective-permute-start | bytes 1179656 | tf_op jit(solution)/shard_map/ppermute | solution.py:254
  20.6 0.0 collective-permute-done.5.refs_2_
  20.6 1.6 %collective-permute-done.4.refs_1_ = bf16[1,3,512,128]{3,2,1,0:T(8,128)(2,1)S(1)} collective-permute-done((bf16[1,3,512,128]{3,2,1,0:T(8,128)(2,1)S(1)}, bf16[1,3,512,128]{3,2,1,0:T(8,128)(2,1)S(1)}, u32[]{:S(2)}, u32[]{:S(2)}) %collective-permute-start.4) | collective-permute-done | bytes 393248 | tf_op jit(solution)/shard_map/ppermute | solution.py:254
  22.2 12.7 %convnext_first.3 = (bf16[1,8,32,8,256]{4,3,2,1,0:T(8,128)(2,1)S(1)}, bf16[1,3,32,8,256]{4,3,2,1,0:T(8,128)(2,1)S(1)}, bf16[1,3,32,8,256]{4,3,2,1,0:T(8,128)(2,1)S(1)}) custom-call(bf16[2,8,512,128]{3,2,1,0:T(8,128)(2,1)S(1)} %copy-done, bf16[1,3,512,128]{3,2,1,0:T(8,128)(2,1)S(1)} %collective-permute-done.4.refs_1_, ...), custom_call_target="tpu_custom_call" | custom-call | flops 1125122048 | bytes 2097152 | tf_op jit(solution)/shard_map/convnext_first/pallas_call | solution.py:172
  34.9 0.0 copy-start.6
  34.9 1.9 %collective-permute-start.6 = (bf16[1,3,32,8,256]{4,3,2,1,0:T(8,128)(2,1)S(1)}, bf16[1,3,32,8,256]{4,3,2,1,0:T(8,128)(2,1)S(1)}, u32[]{:S(2)}, u32[]{:S(2)}) collective-permute-start(bf16[1,3,32,8,256]{4,3,2,1,0:T(8,128)(2,1)S(1)} %get-tuple-element.18), channel_id=1, source_target_pairs={{0,1},{1,2},{2,3},{3,4},{4,5},{5,6},{6,7},{7,8},{8,9},{9,10},{10,1... | collective-permute-start | bytes 1179656 | tf_op jit(solution)/shard_map/ppermute | solution.py:260
  36.9 7.3 %collective-permute-start.7 = (bf16[1,3,32,8,256]{4,3,2,1,0:T(8,128)(2,1)S(1)}, bf16[1,3,32,8,256]{4,3,2,1,0:T(8,128)(2,1)S(1)}, u32[]{:S(2)}, u32[]{:S(2)}) collective-permute-start(bf16[1,3,32,8,256]{4,3,2,1,0:T(8,128)(2,1)S(1)} %get-tuple-element.19), channel_id=1, source_target_pairs={{1,0},{2,1},{3,2},{4,3},{5,4},{6,5},{7,6},{8,7},{9,8},{10,9},{11,1... | collective-permute-start | bytes 1179656 | tf_op jit(solution)/shard_map/ppermute | solution.py:260
  44.1 0.0 collective-permute-done.refs_1_
  44.2 12.7 %convnext_first.2 = (bf16[1,8,32,8,256]{4,3,2,1,0:T(8,128)(2,1)S(1)}, bf16[1,3,32,8,256]{4,3,2,1,0:T(8,128)(2,1)S(1)}, bf16[1,3,32,8,256]{4,3,2,1,0:T(8,128)(2,1)S(1)}) custom-call(bf16[2,8,512,128]{3,2,1,0:T(8,128)(2,1)S(1)} %copy-done, bf16[1,3,512,128]{3,2,1,0:T(8,128)(2,1)S(1)} %collective-permute-done.refs_1_, ...), custom_call_target="tpu_custom_call" | custom-call | flops 1125122048 | bytes 2097152 | tf_op jit(solution)/shard_map/convnext_first/pallas_call | solution.py:172
  56.9 1.9 %collective-permute-start.2 = (bf16[1,3,32,8,256]{4,3,2,1,0:T(8,128)(2,1)S(1)}, bf16[1,3,32,8,256]{4,3,2,1,0:T(8,128)(2,1)S(1)}, u32[]{:S(2)}, u32[]{:S(2)}) collective-permute-start(bf16[1,3,32,8,256]{4,3,2,1,0:T(8,128)(2,1)S(1)} %get-tuple-element.15), channel_id=1, source_target_pairs={{0,1},{1,2},{2,3},{3,4},{4,5},{5,6},{6,7},{7,8},{8,9},{9,10},{10,1... | collective-permute-start | bytes 1179656 | tf_op jit(solution)/shard_map/ppermute | solution.py:260
  58.8 7.3 %collective-permute-start.3 = (bf16[1,3,32,8,256]{4,3,2,1,0:T(8,128)(2,1)S(1)}, bf16[1,3,32,8,256]{4,3,2,1,0:T(8,128)(2,1)S(1)}, u32[]{:S(2)}, u32[]{:S(2)}) collective-permute-start(bf16[1,3,32,8,256]{4,3,2,1,0:T(8,128)(2,1)S(1)} %get-tuple-element.16), channel_id=1, source_target_pairs={{1,0},{2,1},{3,2},{4,3},{5,4},{6,5},{7,6},{8,7},{9,8},{10,9},{11,1... | collective-permute-start | bytes 1179656 | tf_op jit(solution)/shard_map/ppermute | solution.py:260
  66.1 0.0 collective-permute-done.7.refs_2_
  66.1 12.1 %convnext_last.2 = (bf16[2,8,512,128]{3,2,1,0:T(8,128)(2,1)}, f32[1,64,128]{2,1,0:T(8,128)S(1)}, bf16[1,64,128]{2,1,0:T(8,128)(2,1)S(1)}) custom-call(bf16[1,8,32,8,256]{4,3,2,1,0:T(8,128)(2,1)S(1)} %get-tuple-element.17.refs_0_, bf16[1,3,32,8,256]{4,3,2,1,0:T(8,128)(2,1)S(1)} %collective-permute-done.6.refs_1_, ...), custom_call_target="tpu_custom_call" | custom-call | flops 1125122048 | bytes 2097152 | tf_op jit(solution)/shard_map/convnext_last/pallas_call | solution.py:172
  78.2 12.1 %convnext_last.3 = (bf16[2,8,512,128]{3,2,1,0:T(8,128)(2,1)}, f32[1,64,128]{2,1,0:T(8,128)S(1)}, bf16[1,64,128]{2,1,0:T(8,128)(2,1)S(1)}) custom-call(bf16[1,8,32,8,256]{4,3,2,1,0:T(8,128)(2,1)S(1)} %get-tuple-element.14.refs_0_, bf16[1,3,32,8,256]{4,3,2,1,0:T(8,128)(2,1)S(1)} %collective-permute-done.2.refs_1_, ...), custom_call_target="tpu_custom_call", output_to_operand_aliasing={{0}: (10, {})} | custom-call | flops 1125122048 | bytes 2097152 | tf_op jit(solution)/shard_map/convnext_last/pallas_call | solution.py:172
  90.3 0.8 broadcast_in_dim.3
  91.1 6.0 %all-to-all-start = ((bf16[8,2,64,128]{3,2,1,0:T(8,128)(2,1)}), bf16[8,2,64,128]{3,2,1,0:T(8,128)(2,1)S(1)}, u32[]{:S(2)}, u32[]{:S(2)}) async-start(bf16[8,2,64,128]{3,2,1,0:T(8,128)(2,1)} %broadcast_in_dim.3), calls=%async_computation | async-start | bytes 524288 | tf_op jit(solution)/shard_map/all_to_all | solution.py:242
  97.1 0.6 pad_maximum_fusion.pool_ref
  97.7 6.7 %all-to-all-done = bf16[8,2,64,128]{3,2,1,0:T(8,128)(2,1)S(1)} async-done(((bf16[8,2,64,128]{3,2,1,0:T(8,128)(2,1)}), bf16[8,2,64,128]{3,2,1,0:T(8,128)(2,1)S(1)}, u32[]{:S(2)}, u32[]{:S(2)}) %all-to-all-start) | async-done | bytes 262176 | tf_op jit(solution)/shard_map/all_to_all | solution.py:242
  104.4 0.7 copy-done.7
  105.1 2.6 %member_attention.1 = bf16[2,1,64,128]{3,2,1,0:T(8,128)(2,1)} custom-call(bf16[16,64,128]{2,1,0:T(8,128)(2,1)} %bitcast.4, bf16[2,64,128]{2,1,0:T(8,128)(2,1)} %copy-done.8, f32[2,64,128]{2,1,0:T(8,128)} %pad_maximum_fusion.pool_ref, bf16[128,384]{1,0:T(8,128)(2,1)} %wqkv_ref.1, bf16[128,128]{1,0:T(8,128)(2,1)} %wproj_ref.1), custom_call_target="tpu_custom_call" | custom-call | tf_op jit(solution)/shard_map/member_attention/pallas_call | solution.py:230
  (25 shorter events, 0.1 us)
Async XLA Ops:
  0.6 21.5 %copy-start = (bf16[2,8,512,128]{3,2,1,0:T(8,128)(2,1)S(1)}, bf16[2,8,512,128]{3,2,1,0:T(8,128)(2,1)}, u32[]{:S(2)}) copy-start(bf16[2,8,512,128]{3,2,1,0:T(8,128)(2,1)} %refs_0_.3) | copy-start | bytes 6291460
  0.6 19.9 %copy-start.9 = (f32[2,7,7,128]{3,0,2,1:T(2,128)S(1)}, f32[2,7,7,128]{3,0,2,1:T(2,128)}, u32[]{:S(2)}) copy-start(f32[2,7,7,128]{3,0,2,1:T(2,128)} %param.11) | copy-start | bytes 150532
  0.7 21.5 %copy-start.2 = (bf16[2,512,128]{2,1,0:T(8,128)(2,1)S(1)}, bf16[2,512,128]{2,1,0:T(8,128)(2,1)}, u32[]{:S(2)}) copy-start(bf16[2,512,128]{2,1,0:T(8,128)(2,1)} %refs_8_.7) | copy-start | bytes 786436
  0.7 21.5 %copy-start.3 = (f32[2,512]{1,0:T(2,128)S(1)}, f32[2,512]{1,0:T(2,128)}, u32[]{:S(2)}) copy-start(f32[2,512]{1,0:T(2,128)} %refs_7_.7) | copy-start | bytes 12292
  0.7 21.5 %copy-start.1 = (bf16[2,128,512]{2,1,0:T(8,128)(2,1)S(1)}, bf16[2,128,512]{2,1,0:T(8,128)(2,1)}, u32[]{:S(2)}) copy-start(bf16[2,128,512]{2,1,0:T(8,128)(2,1)} %refs_6_.7) | copy-start | bytes 786436
  0.7 21.5 %copy-start.5 = (f32[2,128]{1,0:T(2,128)S(1)}, f32[2,128]{1,0:T(2,128)}, u32[]{:S(2)}) copy-start(f32[2,128]{1,0:T(2,128)} %refs_5_.7) | copy-start | bytes 3076
  0.7 21.5 %copy-start.4 = (f32[2,128]{1,0:T(2,128)S(1)}, f32[2,128]{1,0:T(2,128)}, u32[]{:S(2)}) copy-start(f32[2,128]{1,0:T(2,128)} %refs_4_.7) | copy-start | bytes 3076
  2.3 18.3 %collective-permute-start.5 = (bf16[1,3,512,128]{3,2,1,0:T(8,128)(2,1)S(1)}, bf16[1,3,512,128]{3,2,1,0:T(8,128)(2,1)S(1)}, u32[]{:S(2)}, u32[]{:S(2)}) collective-permute-start(bf16[1,3,512,128]{3,2,1,0:T(8,128)(2,1)S(1)} %get-tuple-element.26), channel_id=1, source_target_pairs={{1,0},{2,1},{3,2},{4,3},{5,4},{6,5},{7,6},{8,7},{9,8},{10,9},{11,1... | collective-permute-start | bytes 1179656 | tf_op jit(solution)/shard_map/ppermute | solution.py:255
  9.5 12.7 %collective-permute-start.4 = (bf16[1,3,512,128]{3,2,1,0:T(8,128)(2,1)S(1)}, bf16[1,3,512,128]{3,2,1,0:T(8,128)(2,1)S(1)}, u32[]{:S(2)}, u32[]{:S(2)}) collective-permute-start(bf16[1,3,512,128]{3,2,1,0:T(8,128)(2,1)S(1)} %get-tuple-element.27), channel_id=1, source_target_pairs={{0,1},{1,2},{2,3},{3,4},{4,5},{5,6},{6,7},{7,8},{8,9},{9,10},{10,1... | collective-permute-start | bytes 1179656 | tf_op jit(solution)/shard_map/ppermute | solution.py:254
  11.4 32.7 %collective-permute-start.1 = (bf16[1,3,512,128]{3,2,1,0:T(8,128)(2,1)S(1)}, bf16[1,3,512,128]{3,2,1,0:T(8,128)(2,1)S(1)}, u32[]{:S(2)}, u32[]{:S(2)}) collective-permute-start(bf16[1,3,512,128]{3,2,1,0:T(8,128)(2,1)S(1)} %get-tuple-element.28), channel_id=1, source_target_pairs={{1,0},{2,1},{3,2},{4,3},{5,4},{6,5},{7,6},{8,7},{9,8},{10,9},{11,1... | collective-permute-start | bytes 1179656 | tf_op jit(solution)/shard_map/ppermute | solution.py:255
  18.7 25.5 %collective-permute-start = (bf16[1,3,512,128]{3,2,1,0:T(8,128)(2,1)S(1)}, bf16[1,3,512,128]{3,2,1,0:T(8,128)(2,1)S(1)}, u32[]{:S(2)}, u32[]{:S(2)}) collective-permute-start(bf16[1,3,512,128]{3,2,1,0:T(8,128)(2,1)S(1)} %get-tuple-element.29), channel_id=1, source_target_pairs={{0,1},{1,2},{2,3},{3,4},{4,5},{5,6},{6,7},{7,8},{8,9},{9,10},{10,1... | collective-permute-start | bytes 1179656 | tf_op jit(solution)/shard_map/ppermute | solution.py:254
  34.9 31.2 %copy-start.6 = (f32[128]{0:T(128)S(1)}, f32[128]{0:T(128)}, u32[]{:S(2)}) copy-start(f32[128]{0:T(128)} %param.17) | copy-start | bytes 1540
  34.9 31.1 %collective-permute-start.6 = (bf16[1,3,32,8,256]{4,3,2,1,0:T(8,128)(2,1)S(1)}, bf16[1,3,32,8,256]{4,3,2,1,0:T(8,128)(2,1)S(1)}, u32[]{:S(2)}, u32[]{:S(2)}) collective-permute-start(bf16[1,3,32,8,256]{4,3,2,1,0:T(8,128)(2,1)S(1)} %get-tuple-element.18), channel_id=1, source_target_pairs={{0,1},{1,2},{2,3},{3,4},{4,5},{5,6},{6,7},{7,8},{8,9},{9,10},{10,1... | collective-permute-start | bytes 1179656 | tf_op jit(solution)/shard_map/ppermute | solution.py:260
  36.9 29.2 %collective-permute-start.7 = (bf16[1,3,32,8,256]{4,3,2,1,0:T(8,128)(2,1)S(1)}, bf16[1,3,32,8,256]{4,3,2,1,0:T(8,128)(2,1)S(1)}, u32[]{:S(2)}, u32[]{:S(2)}) collective-permute-start(bf16[1,3,32,8,256]{4,3,2,1,0:T(8,128)(2,1)S(1)} %get-tuple-element.19), channel_id=1, source_target_pairs={{1,0},{2,1},{3,2},{4,3},{5,4},{6,5},{7,6},{8,7},{9,8},{10,9},{11,1... | collective-permute-start | bytes 1179656 | tf_op jit(solution)/shard_map/ppermute | solution.py:260
  56.9 21.3 %collective-permute-start.2 = (bf16[1,3,32,8,256]{4,3,2,1,0:T(8,128)(2,1)S(1)}, bf16[1,3,32,8,256]{4,3,2,1,0:T(8,128)(2,1)S(1)}, u32[]{:S(2)}, u32[]{:S(2)}) collective-permute-start(bf16[1,3,32,8,256]{4,3,2,1,0:T(8,128)(2,1)S(1)} %get-tuple-element.15), channel_id=1, source_target_pairs={{0,1},{1,2},{2,3},{3,4},{4,5},{5,6},{6,7},{7,8},{8,9},{9,10},{10,1... | collective-permute-start | bytes 1179656 | tf_op jit(solution)/shard_map/ppermute | solution.py:260
  58.8 19.4 %collective-permute-start.3 = (bf16[1,3,32,8,256]{4,3,2,1,0:T(8,128)(2,1)S(1)}, bf16[1,3,32,8,256]{4,3,2,1,0:T(8,128)(2,1)S(1)}, u32[]{:S(2)}, u32[]{:S(2)}) collective-permute-start(bf16[1,3,32,8,256]{4,3,2,1,0:T(8,128)(2,1)S(1)} %get-tuple-element.16), channel_id=1, source_target_pairs={{1,0},{2,1},{3,2},{4,3},{5,4},{6,5},{7,6},{8,7},{9,8},{10,9},{11,1... | collective-permute-start | bytes 1179656 | tf_op jit(solution)/shard_map/ppermute | solution.py:260
  90.3 14.1 %copy-start.8 = (bf16[2,64,128]{2,1,0:T(8,128)(2,1)}, bf16[2,64,128]{2,1,0:T(8,128)(2,1)S(1)}, u32[]{:S(2)}) copy-start(bf16[2,64,128]{2,1,0:T(8,128)(2,1)S(1)} %constant_dynamic-update-slice_fusion.own_ref) | copy-start | bytes 98308
  91.1 13.3 %all-to-all-start = ((bf16[8,2,64,128]{3,2,1,0:T(8,128)(2,1)}), bf16[8,2,64,128]{3,2,1,0:T(8,128)(2,1)S(1)}, u32[]{:S(2)}, u32[]{:S(2)}) async-start(bf16[8,2,64,128]{3,2,1,0:T(8,128)(2,1)} %broadcast_in_dim.3), calls=%async_computation | async-start | bytes 524288 | tf_op jit(solution)/shard_map/all_to_all | solution.py:242
  104.4 0.7 copy-start.7
